TPU v7x, 128 devices: a whole 4x4x4 slice. The times are simulated.
128 devices in a mesh: space: 8 (over x_hi, z), rep: 16 (over y, x_lo, core).
Axes of the slice: x: 4 (x_hi: 2, x_lo: 2; x = x_hi * 2 + x_lo), y: 4, z: 4, core: 2. Of those that a mesh axis runs over, the one named last changes fastest.
Arguments:
- features: bfloat16 [16, 40, 96, 1024], P('rep', 'space'), may hold values from -4 to 4.5
- labels: int32 [16, 40, 96], P('rep', 'space'), may hold values from 0 to 2
- w_in: bfloat16 [29, 1024, 256], replicated, may hold values from -0.0625 to 0.0625
- w_proj: bfloat16 [1280, 256], replicated, may hold values from -0.15625 to 0.15625
- w_cls: bfloat16 [256, 3], replicated, may hold values from -0.375 to 0.375
- class_weight: float32 [3], replicated, may hold values from 0.5 to 4
- matching: int32 [16], replicated, may hold values from 0 to 15, as said below
Outputs:
- avg_in: float32 [16, 29696, 256], P('rep', 'space')
- avg_proj: float32 [16, 1280, 256], P('rep', 'space')
- avg_cls: float32 [16, 256, 3], P('rep', 'space')
Inputs may be any that keep to these rules, and one draw needn't show every extreme that they name: matching[i] = i XOR matching[0] with matching[0] nonzero, so replicas are matched in pairs.
All inputs are finite; a program needn't handle non-finite values.
Results may differ from a plain program's by a relative error of at most 0.025.
The roundings to bfloat16 on the way count: a program that leaves them out, or rounds other values in their place, can miss the bound.
Values may be sent and summed in bfloat16 or wider, within the bound.
A program may use at most 256 MiB of HBM per device.

v0:
```python
import jax
import jax.numpy as jnp
from jax import lax
from jax.sharding import PartitionSpec as P

loss_scale = 1024.0


def from_partner(value, axis, apart):
    mask = 2**apart
    pairs = [(source, source ^ mask) for source in range(lax.axis_size(axis))]
    return lax.ppermute(value, axis, pairs)


def shifted(values, offset, along):
    length = values.shape[along]
    extent = abs(offset)
    padding = [(0, 0)] * values.ndim
    padding[along] = (extent, extent)
    return lax.slice_in_dim(
        jnp.pad(values, padding), extent + offset, extent + offset + length, axis=along
    )


def contract(left, right):
    return lax.dot_general(
        left, right, (((0,), (0,)), ((), ())), preferred_element_type=jnp.float32
    )


def per_device(features, labels, w_in, w_proj, w_cls, class_weight, matching):
    field_map = features[0]
    label_map = labels[0]
    rows_dev, col_count, in_width = field_map.shape
    out_width = w_proj.shape[1]
    space_size = lax.axis_size("space")
    space_index = lax.axis_index("space")
    pixels = rows_dev * col_count
    total_pix = pixels * space_size
    flat_rows = field_map.reshape(pixels, in_width)
    column_sum = jnp.sum(field_map, axis=(0, 1), dtype=jnp.float32)
    mean_in = (lax.psum(column_sum, "space") / total_pix).astype(jnp.bfloat16)
    offsets = [-36, -24, -12, 12, 24, 36]
    whole_map = None
    whole_map = lax.all_gather(field_map, "space", axis=0, tiled=True)
    padded = jnp.pad(whole_map, ((36, 36), (0, 0), (0, 0)))
    row_views = {
        offset: lax.dynamic_slice_in_dim(padded, space_index * rows_dev + 36 + offset, rows_dev, 0)
        for offset in offsets
    }
    row_views[0] = field_map
    pre_list = [jnp.dot(flat_rows, w_in[0], preferred_element_type=jnp.float32)]
    for k in range(1, 4):
        dilation = 12 * k
        pre_act = jnp.zeros((rows_dev, col_count, out_width), jnp.float32)
        for i in range(3):
            row_block = row_views[(i - 1) * dilation].reshape(pixels, in_width)
            for j in range(3):
                product = jnp.dot(
                    row_block, w_in[1 + 9 * (k - 1) + 3 * i + j], preferred_element_type=jnp.float32
                )
                pre_act = pre_act + shifted(
                    product.reshape(rows_dev, col_count, out_width), (j - 1) * dilation, 1
                )
        pre_list.append(pre_act.reshape(pixels, out_width))
    pool_pre = jnp.dot(mean_in[None, :], w_in[28], preferred_element_type=jnp.float32)
    act_list = [jax.nn.relu(p).astype(jnp.bfloat16) for p in pre_list]
    pool_act = jnp.broadcast_to(jax.nn.relu(pool_pre).astype(jnp.bfloat16), (pixels, out_width))
    concat = jnp.concatenate(act_list + [pool_act], axis=1)
    y_pre = jnp.dot(concat, w_proj, preferred_element_type=jnp.float32)
    y_act = jax.nn.relu(y_pre).astype(jnp.bfloat16)
    logits = jnp.dot(y_act, w_cls, preferred_element_type=jnp.float32)
    exp_logits = jnp.exp(logits)
    softmax_out = exp_logits / jnp.sum(exp_logits, axis=1, keepdims=True)
    onehot = (
        label_map.reshape(pixels)[:, None] == jnp.arange(logits.shape[1], dtype=jnp.int32)[None, :]
    ).astype(jnp.float32)
    weight = jnp.sum(onehot * class_weight[None, :], axis=1)
    d_logits = ((softmax_out - onehot) * weight[:, None] * (loss_scale / total_pix)).astype(
        jnp.bfloat16
    )
    g_cls = contract(y_act, d_logits)
    d_y = (jnp.dot(d_logits, w_cls.T, preferred_element_type=jnp.float32) * (y_pre > 0)).astype(
        jnp.bfloat16
    )
    g_proj = contract(concat, d_y)
    d_cat = jnp.dot(d_y, w_proj.T, preferred_element_type=jnp.float32)
    d_list = []
    for k in range(4):
        d_branch = (d_cat[:, k * out_width : (k + 1) * out_width] * (pre_list[k] > 0)).astype(
            jnp.bfloat16
        )
        d_list.append(d_branch.reshape(rows_dev, col_count, out_width))
    s_pool = jnp.sum(d_cat[:, 4 * out_width :] * (pool_pre > 0), axis=0)
    grad_list = [contract(flat_rows, d_list[0].reshape(pixels, out_width))]
    for k in range(1, 4):
        dilation = 12 * k
        for i in range(3):
            row_block = row_views[(i - 1) * dilation].reshape(pixels, in_width)
            for j in range(3):
                moved_grad = shifted(d_list[k], -(j - 1) * dilation, 1).reshape(pixels, out_width)
                grad_list.append(contract(row_block, moved_grad))
    grad_list.append(mean_in.astype(jnp.float32)[:, None] * s_pool[None, :])
    g_in = jnp.stack(grad_list).reshape(-1, out_width)
    sum_in, sum_proj, sum_cls = (
        lax.psum_scatter(
            g_in.astype(jnp.bfloat16), "space", scatter_dimension=0, tiled=True
        ).astype(jnp.float32),
        lax.psum_scatter(
            g_proj.astype(jnp.bfloat16), "space", scatter_dimension=0, tiled=True
        ).astype(jnp.float32),
        lax.psum_scatter(
            g_cls.astype(jnp.bfloat16), "space", scatter_dimension=0, tiled=True
        ).astype(jnp.float32),
    )
    share_in = sum_in.astype(jnp.bfloat16)
    share_proj = sum_proj.astype(jnp.bfloat16)
    share_cls = sum_cls.astype(jnp.bfloat16)
    own_grad = jnp.concatenate(
        [share_in.reshape(-1), share_proj.reshape(-1), share_cls.reshape(-1)]
    )
    pair_bits = matching[0]
    partner_grad = own_grad
    for b in range(lax.axis_size("rep").bit_length() - 1):
        swapped = from_partner(partner_grad, "rep", b)
        bit_on = jnp.bitwise_and(jnp.right_shift(pair_bits, b), 1) == 1
        partner_grad = jnp.where(bit_on, swapped, partner_grad)
    partner_full = partner_grad.astype(jnp.float32)
    averaged = (own_grad.astype(jnp.float32) + partner_full) * 0.5
    size_in = share_in.size
    size_proj = share_proj.size
    avg_in = averaged[:size_in].reshape(share_in.shape)
    avg_proj = averaged[size_in : size_in + size_proj].reshape(share_proj.shape)
    avg_cls = averaged[size_in + size_proj :].reshape(share_cls.shape)
    return (avg_in[None], avg_proj[None], avg_cls[None])


def solution(mesh):
    return jax.shard_map(
        per_device,
        mesh=mesh,
        in_specs=(P("rep", "space", None, None), P("rep", "space", None), P(), P(), P(), P(), P()),
        out_specs=(P("rep", "space", None), P("rep", "space", None), P("rep", "space", None)),
        check_vma=False,
    )
```

profile of v0, /device:TPU:0, one launch (start us, length us, event | category | flops | bytes accessed | tf_op | source)
XLA Modules:
  0.0 638.3 jit_solution(8254590426877515783)
XLA Ops:
  8.7 1.4 convert_reduce_fusion
  10.1 25.7 %psum.7 = f32[1024]{0:T(1024)S(1)} all-reduce(f32[1024]{0:T(1024)S(1)} %convert_reduce_fusion), channel_id=1, replica_groups=mesh['space'=8,'rep'=16] {'space'}, use_global_device_ids=true, to_apply=%region_1.0 | all-reduce | flops 1024 | bytes 8192 | tf_op jit(solution)/shard_map/psum | solution.py:42
  37.8 2.5 fusion.97
  40.4 2.6 fusion.94
  43.0 2.6 fusion.92
  45.5 1.8 fusion.89
  47.3 2.6 fusion.87
  49.9 2.6 fusion.84
  52.4 2.6 fusion.177
  55.0 60.4 %all-gather.3.cloned.1.call-done = bf16[1,40,96,1024]{3,2,0,1:T(8,128)(2,1)} async-done(((bf16[1,5,96,1024]{3,2,0,1:T(8,128)(2,1)}), bf16[1,40,96,1024]{3,2,0,1:T(8,128)(2,1)}) %all-gather.3.cloned.1.call-update) | async-done | bytes 7864336 | tf_op jit(solution)/shard_map/all_gather | solution.py:45
  115.5 3.5 pad_dynamic-slice_fusion
  119.0 2.0 fusion.102
  121.1 1.9 fusion.105
  123.0 1.5 fusion.128
  124.5 1.5 fusion.131
  126.0 1.5 fusion.123
  127.4 1.5 fusion.126
  128.9 1.5 fusion.115
  130.4 1.5 fusion.118
  131.9 1.5 fusion.110
  133.4 1.5 fusion.113
  134.9 1.5 fusion.136
  136.4 1.5 fusion.139
  137.9 1.6 fusion.82
  139.5 1.5 fusion.81
  141.0 2.3 maximum_convert_fusion.3
  143.3 1.5 fusion.80
  144.8 1.5 fusion.79
  146.2 1.5 maximum_convert_fusion.2
  147.7 1.5 fusion.78
  149.2 1.5 fusion.77
  150.7 2.3 maximum_convert_fusion.1
  154.2 1.6 convolution_convert_fusion
  155.8 2.0 fusion.186
  159.8 1.3 broadcast_compare_fusion
  161.1 1.6 fusion.173
  162.8 2.5 fusion.13
  165.3 2.6 fusion.67
  167.9 2.5 fusion.15
  170.4 2.5 fusion.65
  176.6 1.3 fusion.63
  181.8 1.3 fusion.25
  185.6 1.3 fusion.29
  188.1 1.3 fusion.55
  189.4 1.3 fusion.33
  190.7 1.3 fusion.53
  192.0 1.3 fusion.51
  193.4 1.3 fusion.35
  194.7 1.3 fusion.49
  195.9 1.3 fusion.37
  202.4 1.3 fusion.43
  203.7 1.3 fusion.45
  206.0 20.5 %copy.70 = bf16[29,1024,256]{2,1,0:T(8,128)(2,1)} copy(bf16[29,1024,256]{1,2,0:T(8,128)(2,1)} %fusion.99) | data formatting | bytes 30408704 | tf_op jit(solution)/shard_map/stack | solution.py:104
  227.9 73.0 %reduce-scatter.8.cloned.1.call-done = bf16[160,256]{1,0:T(8,128)(2,1)} async-done(((bf16[1280,256]{1,0:T(8,128)(2,1)}), bf16[160,256]{1,0:T(8,128)(2,1)}) %reduce-scatter.8.cloned.1.call-update) | async-done | bytes 81936 | tf_op jit(solution)/shard_map/reduce_scatter | solution.py:109
  301.8 177.2 %reduce-scatter.6.cloned.1.call-done = bf16[3712,256]{1,0:T(8,128)(2,1)} async-done(((bf16[29696,256]{1,0:T(8,128)(2,1)}), bf16[3712,256]{1,0:T(8,128)(2,1)}) %reduce-scatter.6.cloned.1.call-update) | async-done | bytes 1900560 | tf_op jit(solution)/shard_map/reduce_scatter | solution.py:106
  479.1 3.5 copy.105
  482.8 3.9 collective-permute-done
  487.7 44.6 %collective-permute-done.1 = bf16[991328]{0:T(1024)(128)(2,1)S(1)} collective-permute-done((bf16[991328]{0:T(1024)(128)(2,1)S(1)}, bf16[991328]{0:T(1024)(128)(2,1)S(1)}, u32[]{:S(2)}, u32[]{:S(2)}) %collective-permute-start.1) | collective-permute-done | bytes 1982688 | tf_op jit(solution)/shard_map/ppermute | solution.py:12
  532.5 1.6 collective-permute-start.2
  534.2 42.9 %collective-permute-done.2 = bf16[991328]{0:T(1024)(128)(2,1)S(1)} collective-permute-done((bf16[991328]{0:T(1024)(128)(2,1)S(1)}, bf16[991328]{0:T(1024)(128)(2,1)S(1)}, u32[]{:S(2)}, u32[]{:S(2)}) %collective-permute-start.2) | collective-permute-done | bytes 1982688 | tf_op jit(solution)/shard_map/ppermute | solution.py:12
  577.3 3.1 collective-permute-start.3
  580.4 41.9 %collective-permute-done.3 = bf16[991328]{0:T(1024)(128)(2,1)S(1)} collective-permute-done((bf16[991328]{0:T(1024)(128)(2,1)S(1)}, bf16[991328]{0:T(1024)(128)(2,1)S(1)}, u32[]{:S(2)}, u32[]{:S(2)}) %collective-permute-start.3) | collective-permute-done | bytes 1982688 | tf_op jit(solution)/shard_map/ppermute | solution.py:12
  623.2 2.1 slice.265
  626.0 5.0 broadcast_in_dim_reshape.9
  (100 shorter events, 30.6 us)
Async XLA Ops:
  7.2 145.9 %copy-start = (bf16[1280,256]{1,0:T(8,128)(2,1)S(1)}, bf16[1280,256]{1,0:T(8,128)(2,1)}, u32[]{:S(2)}) copy-start(bf16[1280,256]{1,0:T(8,128)(2,1)} %param.10) | copy-start | bytes 1966084
  7.2 108.3 %all-gather.3.cloned.1.call-start = ((), (), s32[]{:S(2)}) async-start(), calls=%async_computation.5 | async-start | bytes 8847360 | tf_op jit(solution)/shard_map/all_gather | solution.py:45
  7.9 219.2 %reduce-scatter.10.cloned.1.call-start = ((), (), s32[]{:S(2)}) async-start(), calls=%async_computation.6 | async-start | bytes 73728 | tf_op jit(solution)/shard_map/reduce_scatter | solution.py:112
  118.9 22.0 %copy-start.5 = (bf16[5,96,1024]{2,1,0:T(8,128)(2,1)}, bf16[5,96,1024]{2,1,0:T(8,128)(2,1)S(1)}, u32[]{:S(2)}) copy-start(bf16[5,96,1024]{2,1,0:T(8,128)(2,1)S(1)} %get-tuple-element.15) | copy-start | bytes 2949124
  119.0 22.0 %copy-start.11 = (bf16[5,96,1024]{2,1,0:T(8,128)(2,1)}, bf16[5,96,1024]{2,1,0:T(8,128)(2,1)S(1)}, u32[]{:S(2)}) copy-start(bf16[5,96,1024]{2,1,0:T(8,128)(2,1)S(1)} %get-tuple-element.19) | copy-start | bytes 2949124
  119.0 24.3 %copy-start.9 = (bf16[5,96,1024]{2,1,0:T(8,128)(2,1)}, bf16[5,96,1024]{2,1,0:T(8,128)(2,1)S(1)}, u32[]{:S(2)}) copy-start(bf16[5,96,1024]{2,1,0:T(8,128)(2,1)S(1)} %get-tuple-element.16) | copy-start | bytes 2949124
  119.0 27.3 %copy-start.3 = (bf16[5,96,1024]{2,1,0:T(8,128)(2,1)}, bf16[5,96,1024]{2,1,0:T(8,128)(2,1)S(1)}, u32[]{:S(2)}) copy-start(bf16[5,96,1024]{2,1,0:T(8,128)(2,1)S(1)} %get-tuple-element.17) | copy-start | bytes 2949124
  119.0 28.7 %copy-start.7 = (bf16[5,96,1024]{2,1,0:T(8,128)(2,1)}, bf16[5,96,1024]{2,1,0:T(8,128)(2,1)S(1)}, u32[]{:S(2)}) copy-start(bf16[5,96,1024]{2,1,0:T(8,128)(2,1)S(1)} %get-tuple-element.18) | copy-start | bytes 2949124
  119.0 18.9 %copy-start.17 = (f32[5,96,256]{2,1,0:T(8,128)S(1)}, f32[5,96,256]{2,1,0:T(8,128)}, u32[]{:S(2)}) copy-start(f32[5,96,256]{2,1,0:T(8,128)} %fusion.97) | copy-start | bytes 1474564
  119.0 20.5 %copy-start.2 = (bf16[1,5,96,1024]{3,2,1,0:T(8,128)(2,1)S(1)}, bf16[1,5,96,1024]{3,2,1,0:T(8,128)(2,1)}, u32[]{:S(2)}) copy-start(bf16[1,5,96,1024]{3,2,1,0:T(8,128)(2,1)} %param.7) | copy-start | bytes 2949124
  119.0 20.5 %copy-start.16 = (f32[5,96,256]{2,1,0:T(8,128)S(1)}, f32[5,96,256]{2,1,0:T(8,128)}, u32[]{:S(2)}) copy-start(f32[5,96,256]{2,1,0:T(8,128)} %fusion.94) | copy-start | bytes 1474564
  123.0 20.3 %copy-start.15 = (f32[5,96,256]{2,1,0:T(8,128)S(1)}, f32[5,96,256]{2,1,0:T(8,128)}, u32[]{:S(2)}) copy-start(f32[5,96,256]{2,1,0:T(8,128)} %fusion.92) | copy-start | bytes 1474564
  130.4 17.4 %copy-start.14 = (f32[5,96,256]{2,1,0:T(8,128)S(1)}, f32[5,96,256]{2,1,0:T(8,128)}, u32[]{:S(2)}) copy-start(f32[5,96,256]{2,1,0:T(8,128)} %fusion.87) | copy-start | bytes 1474564
  133.4 15.8 %copy-start.13 = (f32[5,96,256]{2,1,0:T(8,128)S(1)}, f32[5,96,256]{2,1,0:T(8,128)}, u32[]{:S(2)}) copy-start(f32[5,96,256]{2,1,0:T(8,128)} %fusion.84) | copy-start | bytes 1474564
  137.9 15.1 %copy-start.12 = (bf16[480,1280]{1,0:T(8,128)(2,1)S(1)}, bf16[480,1280]{1,0:T(8,128)(2,1)}, u32[]{:S(2)}) copy-start(bf16[480,1280]{1,0:T(8,128)(2,1)} %get-tuple-element.29) | copy-start | bytes 3686404
  139.5 14.1 %copy-start.18 = (bf16[256,3]{0,1:T(4,128)(2,1)S(1)}, bf16[256,3]{0,1:T(4,128)(2,1)}, u32[]{:S(2)}) copy-start(bf16[256,3]{0,1:T(4,128)(2,1)} %param.11) | copy-start | bytes 4612
  159.7 141.2 %reduce-scatter.8.cloned.1.call-start = ((), (), s32[]{:S(2)}) async-start(), calls=%async_computation.4 | async-start | bytes 737280 | tf_op jit(solution)/shard_map/reduce_scatter | solution.py:109
  159.7 16.9 %copy-start.6 = (bf16[5,96,1024]{2,1,0:T(8,128)(2,1)S(1)}, bf16[5,96,1024]{2,1,0:T(8,128)(2,1)}, u32[]{:S(2)}) copy-start(bf16[5,96,1024]{2,1,0:T(8,128)(2,1)} %copy-done.5) | copy-start | bytes 2949124
  159.7 20.7 %copy-start.10 = (bf16[5,96,1024]{2,1,0:T(8,128)(2,1)S(1)}, bf16[5,96,1024]{2,1,0:T(8,128)(2,1)}, u32[]{:S(2)}) copy-start(bf16[5,96,1024]{2,1,0:T(8,128)(2,1)} %copy-done.9) | copy-start | bytes 2949124
  165.3 22.8 %copy-start.4 = (bf16[5,96,1024]{2,1,0:T(8,128)(2,1)S(1)}, bf16[5,96,1024]{2,1,0:T(8,128)(2,1)}, u32[]{:S(2)}) copy-start(bf16[5,96,1024]{2,1,0:T(8,128)(2,1)} %copy-done.3) | copy-start | bytes 2949124
  172.9 19.2 %copy-start.8 = (bf16[5,96,1024]{2,1,0:T(8,128)(2,1)S(1)}, bf16[5,96,1024]{2,1,0:T(8,128)(2,1)}, u32[]{:S(2)}) copy-start(bf16[5,96,1024]{2,1,0:T(8,128)(2,1)} %copy-done.7) | copy-start | bytes 2949124
  198.5 280.6 %reduce-scatter.6.cloned.1.call-start = ((), (), s32[]{:S(2)}) async-start(), calls=%async_computation.3 | async-start | bytes 17104896 | tf_op jit(solution)/shard_map/reduce_scatter | solution.py:106
  226.4 256.4 %copy-start.19 = (s32[16]{0:T(128)S(1)}, s32[16]{0:T(128)}, u32[]{:S(2)}) copy-start(s32[16]{0:T(128)} %param.13) | copy-start | bytes 196
  482.7 4.1 collective-permute-start
  487.0 45.3 %collective-permute-start.1 = (bf16[991328]{0:T(1024)(128)(2,1)S(1)}, bf16[991328]{0:T(1024)(128)(2,1)S(1)}, u32[]{:S(2)}, u32[]{:S(2)}) collective-permute-start(bf16[991328]{0:T(1024)(128)(2,1)S(1)} %broadcast_select_fusion), channel_id=1, source_target_pairs={{0,2},{1,3},{2,0},{3,1},{4,6},{5,7},{6,4},{7,5},{8,10},{9,11},{10,... | collective-permute-start | bytes 5947976 | tf_op jit(solution)/shard_map/ppermute | solution.py:12
  532.5 44.5 %collective-permute-start.2 = (bf16[991328]{0:T(1024)(128)(2,1)S(1)}, bf16[991328]{0:T(1024)(128)(2,1)S(1)}, u32[]{:S(2)}, u32[]{:S(2)}) collective-permute-start(bf16[991328]{0:T(1024)(128)(2,1)S(1)} %broadcast_select_fusion.1), channel_id=1, source_target_pairs={{0,4},{1,5},{2,6},{3,7},{4,0},{5,1},{6,2},{7,3},{8,12},{9,13},{10,... | collective-permute-start | bytes 5947976 | tf_op jit(solution)/shard_map/ppermute | solution.py:12
  577.1 54.7 %copy-start.1 = (bf16[1280,256]{1,0:T(8,128)(2,1)S(1)}, bf16[1280,256]{1,0:T(8,128)(2,1)}, u32[]{:S(2)}) copy-start(bf16[1280,256]{1,0:T(8,128)(2,1)} %param.10) | copy-start | bytes 1966084
  577.3 45.1 %collective-permute-start.3 = (bf16[991328]{0:T(1024)(128)(2,1)S(1)}, bf16[991328]{0:T(1024)(128)(2,1)S(1)}, u32[]{:S(2)}, u32[]{:S(2)}) collective-permute-start(bf16[991328]{0:T(1024)(128)(2,1)S(1)} %broadcast_select_fusion.2), channel_id=1, source_target_pairs={{0,8},{1,9},{2,10},{3,11},{4,12},{5,13},{6,14},{7,15},{8,0},{9,1},... | collective-permute-start | bytes 5947976 | tf_op jit(solution)/shard_map/ppermute | solution.py:12
Sparse Core Ops, SparseCore 0:
  10.3 105.0 all-gather.2
  159.8 67.2 reduce-scatter.9
  230.7 70.1 reduce-scatter.7
  305.1 173.8 reduce-scatter.5
where the time goes:
time: 641 us; the launch traced here: 638 us
  waiting for transfers between devices  445 us (69%)
  matrix products  97.5 us (15%)
  local copies, waits for them, and re-layouts  39.1 us (6%)
  blocking collectives  25.7 us (4%)
  between operations  14.5 us (2%)
  other arithmetic  10.3 us (2%)
    reduce_scatter x1, waiting for transfers between devices, per_device(): lax.psum_scatter(g_in.astype(jnp.bfloat16), 'space', scatter_dimension=0,...  177 us
    ppermute x4, waiting for transfers between devices, from_partner(): return lax.ppermute(value, axis, pairs)  133 us
    reduce_scatter x1, waiting for transfers between devices, per_device(): lax.psum_scatter(g_proj.astype(jnp.bfloat16), 'space', scatter_dimension=...  73 us
    all_gather x1, waiting for transfers between devices, per_device(): whole_map = lax.all_gather(field_map, 'space', axis=0, tiled=True)  60.4 us
    dot_general x27, matrix products, per_device(): jnp.dot(row_block, w_in[1 + 9 * (k - 1) + 3 * i + j], preferred_element_t...  48.2 us
    dot_general x30, matrix products, contract(): lax.dot_general(left, right, (((0,), (0,)), ((), ())), preferred_element_...  42.5 us
    psum x1, blocking collectives, per_device(): mean_in = (lax.psum(column_sum, 'space') / total_pix).astype(jnp.bfloat16)  25.7 us
    another operation x1, local copies, waits for them, and re-layouts, per_device(): g_in = jnp.stack(grad_list).reshape(-1, out_width)  20.5 us
  transfers between devices with their start and end apart: 8, of which 8 were waited for; matrix products, arithmetic and copies ran while one was open for 14% of the time, Pallas kernels for 0%

commit v1 on v0

--- a/solution.py
+++ b/solution.py
@@ -39,7 +39,9 @@
     total_pix = pixels * space_size
     flat_rows = field_map.reshape(pixels, in_width)
     column_sum = jnp.sum(field_map, axis=(0, 1), dtype=jnp.float32)
-    mean_in = (lax.psum(column_sum, "space") / total_pix).astype(jnp.bfloat16)
+    mean_in = (jnp.sum(lax.all_gather(column_sum, "space"), axis=0) / total_pix).astype(
+        jnp.bfloat16
+    )
     offsets = [-36, -24, -12, 12, 24, 36]
     whole_map = None
     whole_map = lax.all_gather(field_map, "space", axis=0, tiled=True)

time: 641 us -> 641 us (level)
  blocking collectives: 25.7 us -> 35.4 us
  waiting for transfers between devices: 445 us -> 436 us
    all_gather x0 -> x1, blocking collectives: none -> 35.4 us  [per_device(): lax.all_gather(column_sum, 'space')]
    psum x1 -> x0, blocking collectives: 25.7 us -> none  [per_device(): mean_in = (lax.psum(column_sum, 'space') / total_pix).astype(jnp.bfloat16)]
    all_gather x1, waiting for transfers between devices: 60.4 us -> 50.5 us  [per_device(): whole_map = lax.all_gather(field_map, 'space', axis=0, tiled=True)]
where the time goes in v1:
time: 641 us; the launch traced here: 638 us
  waiting for transfers between devices  436 us (68%)
  matrix products  97.7 us (15%)
  local copies, waits for them, and re-layouts  39.1 us (6%)
  blocking collectives  35.4 us (6%)
  between operations  14.5 us (2%)
  other arithmetic  10.3 us (2%)
    reduce_scatter x1, waiting for transfers between devices, per_device(): lax.psum_scatter(g_in.astype(jnp.bfloat16), 'space', scatter_dimension=0,...  177 us
    ppermute x4, waiting for transfers between devices, from_partner(): return lax.ppermute(value, axis, pairs)  133 us
    reduce_scatter x1, waiting for transfers between devices, per_device(): lax.psum_scatter(g_proj.astype(jnp.bfloat16), 'space', scatter_dimension=...  73 us
    all_gather x1, waiting for transfers between devices, per_device(): whole_map = lax.all_gather(field_map, 'space', axis=0, tiled=True)  50.5 us
    dot_general x27, matrix products, per_device(): jnp.dot(row_block, w_in[1 + 9 * (k - 1) + 3 * i + j], preferred_element_t...  48.4 us
    dot_general x30, matrix products, contract(): lax.dot_general(left, right, (((0,), (0,)), ((), ())), preferred_element_...  42.3 us
    all_gather x1, blocking collectives, per_device(): lax.all_gather(column_sum, 'space')  35.4 us
    another operation x1, local copies, waits for them, and re-layouts, per_device(): g_in = jnp.stack(grad_list).reshape(-1, out_width)  20.5 us
  transfers between devices with their start and end apart: 8, of which 8 were waited for; matrix products, arithmetic and copies ran while one was open for 14% of the time, Pallas kernels for 0%

profile of v1, /device:TPU:0, one launch (start us, length us, event | category | flops | bytes accessed | tf_op | source)
XLA Modules:
  0.0 638.4 jit_solution(9131714183239734756)
XLA Ops:
  8.7 1.4 convert_reduce_fusion
  10.1 35.4 %all-gather.1 = f32[8192]{0:T(1024)S(1)} all-gather(f32[1024]{0:T(1024)S(1)} %convert_reduce_fusion), channel_id=3, replica_groups=mesh['space'=8,'rep'=16] {'space'}, dimensions={0}, use_global_device_ids=true | all-gather | bytes 36864 | tf_op jit(solution)/shard_map/all_gather | solution.py:42
  47.6 2.5 fusion.97
  50.1 2.6 fusion.94
  52.7 2.6 fusion.92
  55.3 2.0 fusion.89
  57.3 2.6 fusion.87
  59.8 2.6 fusion.84
  62.4 2.6 fusion.177
  65.0 50.5 %all-gather.4.cloned.1.call-done = bf16[1,40,96,1024]{3,2,0,1:T(8,128)(2,1)} async-done(((bf16[1,5,96,1024]{3,2,0,1:T(8,128)(2,1)}), bf16[1,40,96,1024]{3,2,0,1:T(8,128)(2,1)}) %all-gather.4.cloned.1.call-update) | async-done | bytes 7864336 | tf_op jit(solution)/shard_map/all_gather | solution.py:47
  115.5 3.5 pad_dynamic-slice_fusion
  119.1 2.0 fusion.102
  121.1 1.9 fusion.105
  123.1 1.5 fusion.128
  124.6 1.5 fusion.131
  126.0 1.5 fusion.123
  127.5 1.5 fusion.126
  129.0 1.5 fusion.115
  130.5 1.5 fusion.118
  132.0 1.5 fusion.110
  133.5 1.5 fusion.113
  135.0 1.5 fusion.136
  136.5 1.5 fusion.139
  138.0 1.6 fusion.82
  139.6 1.5 fusion.81
  141.1 2.3 maximum_convert_fusion.3
  143.4 1.5 fusion.80
  144.8 1.5 fusion.79
  146.3 1.5 maximum_convert_fusion.2
  147.8 1.5 fusion.78
  149.3 1.5 fusion.77
  150.8 2.3 maximum_convert_fusion.1
  154.5 1.4 convolution_convert_fusion
  155.9 2.0 fusion.186
  159.8 1.3 broadcast_compare_fusion
  161.1 1.6 fusion.173
  162.9 2.5 fusion.13
  165.4 2.6 fusion.67
  167.9 2.5 fusion.15
  170.4 2.5 fusion.65
  176.7 1.3 fusion.63
  181.8 1.3 fusion.25
  185.7 1.3 fusion.29
  188.2 1.3 fusion.55
  189.5 1.3 fusion.33
  190.8 1.3 fusion.53
  192.1 1.3 fusion.51
  193.4 1.3 fusion.35
  194.7 1.3 fusion.49
  196.0 1.3 fusion.37
  202.5 1.3 fusion.43
  203.8 1.3 fusion.45
  206.0 20.5 %copy.92 = bf16[29,1024,256]{2,1,0:T(8,128)(2,1)} copy(bf16[29,1024,256]{1,2,0:T(8,128)(2,1)} %fusion.99) | data formatting | bytes 30408704 | tf_op jit(solution)/shard_map/stack | solution.py:106
  228.0 73.0 %reduce-scatter.8.cloned.1.call-done = bf16[160,256]{1,0:T(8,128)(2,1)} async-done(((bf16[1280,256]{1,0:T(8,128)(2,1)}), bf16[160,256]{1,0:T(8,128)(2,1)}) %reduce-scatter.8.cloned.1.call-update) | async-done | bytes 81936 | tf_op jit(solution)/shard_map/reduce_scatter | solution.py:111
  301.9 177.3 %reduce-scatter.6.cloned.1.call-done = bf16[3712,256]{1,0:T(8,128)(2,1)} async-done(((bf16[29696,256]{1,0:T(8,128)(2,1)}), bf16[3712,256]{1,0:T(8,128)(2,1)}) %reduce-scatter.6.cloned.1.call-update) | async-done | bytes 1900560 | tf_op jit(solution)/shard_map/reduce_scatter | solution.py:108
  479.2 3.5 copy.127
  483.0 3.9 collective-permute-done
  487.8 44.6 %collective-permute-done.1 = bf16[991328]{0:T(1024)(128)(2,1)S(1)} collective-permute-done((bf16[991328]{0:T(1024)(128)(2,1)S(1)}, bf16[991328]{0:T(1024)(128)(2,1)S(1)}, u32[]{:S(2)}, u32[]{:S(2)}) %collective-permute-start.1) | collective-permute-done | bytes 1982688 | tf_op jit(solution)/shard_map/ppermute | solution.py:12
  532.7 1.6 collective-permute-start.2
  534.3 42.9 %collective-permute-done.2 = bf16[991328]{0:T(1024)(128)(2,1)S(1)} collective-permute-done((bf16[991328]{0:T(1024)(128)(2,1)S(1)}, bf16[991328]{0:T(1024)(128)(2,1)S(1)}, u32[]{:S(2)}, u32[]{:S(2)}) %collective-permute-start.2) | collective-permute-done | bytes 1982688 | tf_op jit(solution)/shard_map/ppermute | solution.py:12
  577.4 3.1 collective-permute-start.3
  580.5 42.0 %collective-permute-done.3 = bf16[991328]{0:T(1024)(128)(2,1)S(1)} collective-permute-done((bf16[991328]{0:T(1024)(128)(2,1)S(1)}, bf16[991328]{0:T(1024)(128)(2,1)S(1)}, u32[]{:S(2)}, u32[]{:S(2)}) %collective-permute-start.3) | collective-permute-done | bytes 1982688 | tf_op jit(solution)/shard_map/ppermute | solution.py:12
  623.3 2.1 slice.265
  626.1 5.0 broadcast_in_dim_reshape.9
  (102 shorter events, 30.7 us)
Async XLA Ops:
  7.2 146.0 %copy-start = (bf16[1280,256]{1,0:T(8,128)(2,1)S(1)}, bf16[1280,256]{1,0:T(8,128)(2,1)}, u32[]{:S(2)}) copy-start(bf16[1280,256]{1,0:T(8,128)(2,1)} %param.10) | copy-start | bytes 1966084
  7.2 108.4 %all-gather.4.cloned.1.call-start = ((), (), s32[]{:S(2)}) async-start(), calls=%async_computation.5 | async-start | bytes 8847360 | tf_op jit(solution)/shard_map/all_gather | solution.py:47
  7.9 219.3 %reduce-scatter.10.cloned.1.call-start = ((), (), s32[]{:S(2)}) async-start(), calls=%async_computation.6 | async-start | bytes 73728 | tf_op jit(solution)/shard_map/reduce_scatter | solution.py:114
  119.0 22.0 %copy-start.5 = (bf16[5,96,1024]{2,1,0:T(8,128)(2,1)}, bf16[5,96,1024]{2,1,0:T(8,128)(2,1)S(1)}, u32[]{:S(2)}) copy-start(bf16[5,96,1024]{2,1,0:T(8,128)(2,1)S(1)} %get-tuple-element.18) | copy-start | bytes 2949124
  119.0 22.0 %copy-start.11 = (bf16[5,96,1024]{2,1,0:T(8,128)(2,1)}, bf16[5,96,1024]{2,1,0:T(8,128)(2,1)S(1)}, u32[]{:S(2)}) copy-start(bf16[5,96,1024]{2,1,0:T(8,128)(2,1)S(1)} %get-tuple-element.22) | copy-start | bytes 2949124
  119.1 24.3 %copy-start.9 = (bf16[5,96,1024]{2,1,0:T(8,128)(2,1)}, bf16[5,96,1024]{2,1,0:T(8,128)(2,1)S(1)}, u32[]{:S(2)}) copy-start(bf16[5,96,1024]{2,1,0:T(8,128)(2,1)S(1)} %get-tuple-element.19) | copy-start | bytes 2949124
  119.1 27.3 %copy-start.3 = (bf16[5,96,1024]{2,1,0:T(8,128)(2,1)}, bf16[5,96,1024]{2,1,0:T(8,128)(2,1)S(1)}, u32[]{:S(2)}) copy-start(bf16[5,96,1024]{2,1,0:T(8,128)(2,1)S(1)} %get-tuple-element.20) | copy-start | bytes 2949124
  119.1 28.7 %copy-start.7 = (bf16[5,96,1024]{2,1,0:T(8,128)(2,1)}, bf16[5,96,1024]{2,1,0:T(8,128)(2,1)S(1)}, u32[]{:S(2)}) copy-start(bf16[5,96,1024]{2,1,0:T(8,128)(2,1)S(1)} %get-tuple-element.21) | copy-start | bytes 2949124
  119.1 18.9 %copy-start.17 = (f32[5,96,256]{2,1,0:T(8,128)S(1)}, f32[5,96,256]{2,1,0:T(8,128)}, u32[]{:S(2)}) copy-start(f32[5,96,256]{2,1,0:T(8,128)} %fusion.97) | copy-start | bytes 1474564
  119.1 20.5 %copy-start.2 = (bf16[1,5,96,1024]{3,2,1,0:T(8,128)(2,1)S(1)}, bf16[1,5,96,1024]{3,2,1,0:T(8,128)(2,1)}, u32[]{:S(2)}) copy-start(bf16[1,5,96,1024]{3,2,1,0:T(8,128)(2,1)} %param.7) | copy-start | bytes 2949124
  119.1 20.5 %copy-start.16 = (f32[5,96,256]{2,1,0:T(8,128)S(1)}, f32[5,96,256]{2,1,0:T(8,128)}, u32[]{:S(2)}) copy-start(f32[5,96,256]{2,1,0:T(8,128)} %fusion.94) | copy-start | bytes 1474564
  123.0 20.3 %copy-start.15 = (f32[5,96,256]{2,1,0:T(8,128)S(1)}, f32[5,96,256]{2,1,0:T(8,128)}, u32[]{:S(2)}) copy-start(f32[5,96,256]{2,1,0:T(8,128)} %fusion.92) | copy-start | bytes 1474564
  130.5 17.4 %copy-start.14 = (f32[5,96,256]{2,1,0:T(8,128)S(1)}, f32[5,96,256]{2,1,0:T(8,128)}, u32[]{:S(2)}) copy-start(f32[5,96,256]{2,1,0:T(8,128)} %fusion.87) | copy-start | bytes 1474564
  133.5 15.8 %copy-start.13 = (f32[5,96,256]{2,1,0:T(8,128)S(1)}, f32[5,96,256]{2,1,0:T(8,128)}, u32[]{:S(2)}) copy-start(f32[5,96,256]{2,1,0:T(8,128)} %fusion.84) | copy-start | bytes 1474564
  138.0 15.1 %copy-start.12 = (bf16[480,1280]{1,0:T(8,128)(2,1)S(1)}, bf16[480,1280]{1,0:T(8,128)(2,1)}, u32[]{:S(2)}) copy-start(bf16[480,1280]{1,0:T(8,128)(2,1)} %get-tuple-element.32) | copy-start | bytes 3686404
  139.6 14.1 %copy-start.18 = (bf16[256,3]{0,1:T(4,128)(2,1)S(1)}, bf16[256,3]{0,1:T(4,128)(2,1)}, u32[]{:S(2)}) copy-start(bf16[256,3]{0,1:T(4,128)(2,1)} %param.11) | copy-start | bytes 4612
  159.8 141.2 %reduce-scatter.8.cloned.1.call-start = ((), (), s32[]{:S(2)}) async-start(), calls=%async_computation.4 | async-start | bytes 737280 | tf_op jit(solution)/shard_map/reduce_scatter | solution.py:111
  159.8 16.9 %copy-start.6 = (bf16[5,96,1024]{2,1,0:T(8,128)(2,1)S(1)}, bf16[5,96,1024]{2,1,0:T(8,128)(2,1)}, u32[]{:S(2)}) copy-start(bf16[5,96,1024]{2,1,0:T(8,128)(2,1)} %copy-done.5) | copy-start | bytes 2949124
  159.8 20.7 %copy-start.10 = (bf16[5,96,1024]{2,1,0:T(8,128)(2,1)S(1)}, bf16[5,96,1024]{2,1,0:T(8,128)(2,1)}, u32[]{:S(2)}) copy-start(bf16[5,96,1024]{2,1,0:T(8,128)(2,1)} %copy-done.9) | copy-start | bytes 2949124
  165.4 22.8 %copy-start.4 = (bf16[5,96,1024]{2,1,0:T(8,128)(2,1)S(1)}, bf16[5,96,1024]{2,1,0:T(8,128)(2,1)}, u32[]{:S(2)}) copy-start(bf16[5,96,1024]{2,1,0:T(8,128)(2,1)} %copy-done.3) | copy-start | bytes 2949124
  172.9 19.2 %copy-start.8 = (bf16[5,96,1024]{2,1,0:T(8,128)(2,1)S(1)}, bf16[5,96,1024]{2,1,0:T(8,128)(2,1)}, u32[]{:S(2)}) copy-start(bf16[5,96,1024]{2,1,0:T(8,128)(2,1)} %copy-done.7) | copy-start | bytes 2949124
  198.6 280.6 %reduce-scatter.6.cloned.1.call-start = ((), (), s32[]{:S(2)}) async-start(), calls=%async_computation.3 | async-start | bytes 17104896 | tf_op jit(solution)/shard_map/reduce_scatter | solution.py:108
  226.5 256.4 %copy-start.19 = (s32[16]{0:T(128)S(1)}, s32[16]{0:T(128)}, u32[]{:S(2)}) copy-start(s32[16]{0:T(128)} %param.13) | copy-start | bytes 196
  482.8 4.1 collective-permute-start
  487.1 45.3 %collective-permute-start.1 = (bf16[991328]{0:T(1024)(128)(2,1)S(1)}, bf16[991328]{0:T(1024)(128)(2,1)S(1)}, u32[]{:S(2)}, u32[]{:S(2)}) collective-permute-start(bf16[991328]{0:T(1024)(128)(2,1)S(1)} %broadcast_select_fusion), channel_id=1, source_target_pairs={{0,2},{1,3},{2,0},{3,1},{4,6},{5,7},{6,4},{7,5},{8,10},{9,11},{10,... | collective-permute-start | bytes 5947976 | tf_op jit(solution)/shard_map/ppermute | solution.py:12
  532.7 44.5 %collective-permute-start.2 = (bf16[991328]{0:T(1024)(128)(2,1)S(1)}, bf16[991328]{0:T(1024)(128)(2,1)S(1)}, u32[]{:S(2)}, u32[]{:S(2)}) collective-permute-start(bf16[991328]{0:T(1024)(128)(2,1)S(1)} %broadcast_select_fusion.1), channel_id=1, source_target_pairs={{0,4},{1,5},{2,6},{3,7},{4,0},{5,1},{6,2},{7,3},{8,12},{9,13},{10,... | collective-permute-start | bytes 5947976 | tf_op jit(solution)/shard_map/ppermute | solution.py:12
  577.2 54.7 %copy-start.1 = (bf16[1280,256]{1,0:T(8,128)(2,1)S(1)}, bf16[1280,256]{1,0:T(8,128)(2,1)}, u32[]{:S(2)}) copy-start(bf16[1280,256]{1,0:T(8,128)(2,1)} %param.10) | copy-start | bytes 1966084
  577.4 45.1 %collective-permute-start.3 = (bf16[991328]{0:T(1024)(128)(2,1)S(1)}, bf16[991328]{0:T(1024)(128)(2,1)S(1)}, u32[]{:S(2)}, u32[]{:S(2)}) collective-permute-start(bf16[991328]{0:T(1024)(128)(2,1)S(1)} %broadcast_select_fusion.2), channel_id=1, source_target_pairs={{0,8},{1,9},{2,10},{3,11},{4,12},{5,13},{6,14},{7,15},{8,0},{9,1},... | collective-permute-start | bytes 5947976 | tf_op jit(solution)/shard_map/ppermute | solution.py:12
Sparse Core Ops, SparseCore 0:
  10.3 105.1 all-gather.3
  159.9 67.2 reduce-scatter.9
  230.7 70.1 reduce-scatter.7
  305.2 173.9 reduce-scatter.5
